TPU v7x, 256 devices: a whole 4x4x8 slice. The times are simulated.
256 devices in a mesh: rep: 8 (over y, x_hi), blk: 32 (over z, x_lo, core).
Axes of the slice: x: 4 (x_hi: 2, x_lo: 2; x = x_hi * 2 + x_lo), y: 4, z: 8, core: 2. Of those that a mesh axis runs over, the one named last changes fastest.
Arguments:
- features: bfloat16 [131072, 128], P(('rep', 'blk')), may hold values from -6 to 6
- degrees: int32 [131072], P(('rep', 'blk')), may hold values from 1 to 32
- tile_weights: bfloat16 [8, 32, 320, 128, 128], P('rep', 'blk'), may hold values from 0 to 0.049804688
- tile_rows: int32 [8, 32, 320], P('rep', 'blk'), may hold values from 0 to 127, as said below
- tile_cols: int32 [8, 32, 320], P('rep', 'blk'), may hold values from 0 to 31, as said below
- tile_counts: int32 [8, 32], P('rep', 'blk'), may hold values from 1 to 320, as said below
- weight: bfloat16 [128, 256], replicated, may hold values from -0.5 to 0.5
- layer_bias: float32 [256], replicated, may hold values from -3 to 3
- upstream: bfloat16 [131072, 256], P(('rep', 'blk')), may hold values from -6 to 6
Outputs:
- hidden: bfloat16 [131072, 256], P(('rep', 'blk'))
- feature_grad: bfloat16 [131072, 128], P(('rep', 'blk'))
- weight_grad: float32 [128, 256], replicated
- bias_grad: float32 [256], replicated
Inputs may be any that keep to these rules, and one draw needn't show every extreme that they name: `tile_rows`: the first tile_counts slots of a device hold distinct tiles, ordered by row and then by column; a used row h lies in node block r * 32 + h // 4, whose index h // 4 is within 3 steps of the device's blk index around the loop of 32; unused slots hold the device's own first tile row. `tile_cols`: unused slots hold 0. `tile_counts`: at most 80 used slots of one device lie in the rows of one node block; this and the largest count are both reached by some device in every draw.
All inputs are finite; a program needn't handle non-finite values.
Results may differ from a plain program's by a relative error of at most 0.015.
Values may be sent and summed in bfloat16 or wider, within the bound.
A program may use at most 128 MiB of HBM per device.

v0:
```python
import jax
import jax.numpy as jnp
from jax import lax
from jax.sharding import PartitionSpec as P

REACH = 3


def shifted(value, axis, by):
    length = lax.axis_size(axis)
    return lax.ppermute(value, axis, [(i, (i + by) % length) for i in range(length)])


def node_scale(degrees):
    return 1.0 / jnp.sqrt(degrees.astype(jnp.float32) + 1.0)


def on_device(
    features, degrees, tile_weights, tile_rows, tile_cols, tile_counts, weight, layer_bias, upstream
):
    row_count, feat_width = features.shape
    tile_size = tile_weights.shape[-1]
    slot_total = tile_weights.shape[2]
    row_tiles = row_count // tile_size
    rep_count = lax.axis_size("rep")
    blk_count = lax.axis_size("blk")
    blk_index = lax.axis_index("blk")
    window_blocks = 2 * REACH + 1
    window_tiles = window_blocks * row_tiles
    column_tiles = rep_count * row_tiles
    slot_block = slot_total // (2 * (REACH + 1))
    block_total = slot_total // slot_block
    weights_dev = tile_weights[0, 0]
    rows_dev = tile_rows[0, 0]
    cols_dev = tile_cols[0, 0]
    count_dev = tile_counts[0, 0]
    group_index = rows_dev // row_tiles
    distance = (group_index - blk_index) % blk_count
    distance = jnp.where(distance > blk_count // 2, distance - blk_count, distance)
    window_rows = (distance + REACH) * row_tiles + rows_dev % row_tiles
    slot_ids = jnp.arange(slot_total, dtype=jnp.int32)
    slot_valid = slot_ids < count_dev
    window_seg = jnp.where(slot_valid, window_rows, window_tiles)
    column_seg = jnp.where(slot_valid, cols_dev, column_tiles)

    def tile_pass(source_tiles, gather_index, segment_index, segment_total, pattern):

        def add_block(block_id, running):
            slot_first = block_id * slot_block
            weights_part = lax.dynamic_slice_in_dim(weights_dev, slot_first, slot_block, 0)
            gather_part = lax.dynamic_slice_in_dim(gather_index, slot_first, slot_block, 0)
            segment_part = lax.dynamic_slice_in_dim(segment_index, slot_first, slot_block, 0)
            products = jnp.einsum(
                pattern, weights_part, source_tiles[gather_part], preferred_element_type=jnp.float32
            )
            return (
                running
                + jax.ops.segment_sum(products, segment_part, segment_total + 1)[:segment_total]
            )

        zero_sum = jnp.zeros((segment_total, tile_size, feat_width), jnp.float32)
        return lax.fori_loop(0, block_total, add_block, zero_sum)

    node_norm = node_scale(degrees)
    scaled = (node_norm[:, None] * features.astype(jnp.float32)).astype(jnp.bfloat16)
    source_rows = lax.all_gather(scaled, "rep", axis=0, tiled=True)
    source_tiles = source_rows.reshape(column_tiles, tile_size, feat_width)
    partial_value = tile_pass(source_tiles, cols_dev, window_seg, window_tiles, "tab,tbf->taf")
    partial_value = partial_value.reshape(window_blocks, row_count, feat_width)
    neighbor_sum = partial_value[REACH]
    for offset in range(-REACH, REACH + 1):
        if offset != 0:
            neighbor_sum = neighbor_sum + shifted(
                partial_value[offset + REACH].astype(jnp.bfloat16), "blk", offset
            ).astype(jnp.float32)
    aggregated = (node_norm[:, None] * (neighbor_sum + scaled.astype(jnp.float32))).astype(
        jnp.bfloat16
    )
    pre_act = jnp.dot(aggregated, weight, preferred_element_type=jnp.float32) + layer_bias
    hidden = jax.nn.silu(pre_act).astype(jnp.bfloat16)
    gate_sigmoid = jax.nn.sigmoid(pre_act)
    pre_grad = (
        upstream.astype(jnp.float32)
        * (gate_sigmoid + pre_act * gate_sigmoid * (1.0 - gate_sigmoid))
    ).astype(jnp.bfloat16)
    local_weight = jnp.dot(aggregated.T, pre_grad, preferred_element_type=jnp.float32)
    local_bias = jnp.sum(pre_grad.astype(jnp.float32), axis=0)
    weight_sum, bias_sum = lax.psum((local_weight, local_bias), ("rep", "blk"))
    grad_scale = (row_count * rep_count * blk_count) ** (-0.5)
    scaled_grad = (
        node_norm[:, None] * jnp.dot(pre_grad, weight.T, preferred_element_type=jnp.float32)
    ).astype(jnp.bfloat16)
    window_parts = [scaled_grad] * window_blocks
    for offset in range(-REACH, REACH + 1):
        if offset != 0:
            window_parts[offset + REACH] = shifted(scaled_grad, "blk", -offset)
    grad_tiles = jnp.stack(window_parts).reshape(window_tiles, tile_size, feat_width)
    column_part = tile_pass(grad_tiles, window_rows, column_seg, column_tiles, "tab,taf->tbf")
    column_sum = lax.psum_scatter(
        column_part.reshape(rep_count * row_count, feat_width).astype(jnp.bfloat16),
        "rep",
        scatter_dimension=0,
        tiled=True,
    ).astype(jnp.float32)
    feature_grad = (node_norm[:, None] * (column_sum + scaled_grad.astype(jnp.float32))).astype(
        jnp.bfloat16
    )
    return (hidden, feature_grad, weight_sum * grad_scale, bias_sum * grad_scale)


def solution(mesh):
    placed = (
        P(("rep", "blk"), None),
        P(("rep", "blk")),
        P("rep", "blk", None, None, None),
        P("rep", "blk", None),
        P("rep", "blk", None),
        P("rep", "blk"),
        P(),
        P(),
        P(("rep", "blk"), None),
    )
    return jax.shard_map(
        on_device,
        mesh=mesh,
        in_specs=placed,
        out_specs=(P(("rep", "blk"), None), P(("rep", "blk"), None), P(), P()),
        check_vma=False,
    )
```

profile of v0, /device:TPU:32, one launch (start us, length us, event | category | flops | bytes accessed | tf_op | source)
XLA Modules:
  0.0 557.3 jit_solution(4385618830677992955)
XLA Ops:
  11.8 53.4 %all-gather.2.cloned.1.call-done = bf16[4096,128]{1,0:T(8,128)(2,1)} async-done(((bf16[512,128]{1,0:T(8,128)(2,1)}), bf16[4096,128]{1,0:T(8,128)(2,1)}) %all-gather.2.cloned.1.call-update) | async-done | bytes 1048592 | tf_op jit(solution)/shard_map/all_gather | solution.py:66
  65.2 120.4 %while.28 = (s32[]{:T(128)}, f32[28,128,128]{2,1,0:T(8,128)}, s32[320]{0:T(512)S(1)}, bf16[320,128,128]{2,1,0:T(8,128)(2,1)}, s32[320]{0:T(512)S(1)}, /*index=5*...) while((s32[]{:T(128)}, f32[28,128,128]{2,1,0:T(8,128)}, ...), condition=%wide.region_2.3_spmd.clone, body=%wide.region_0.2_spmd.clone.sunk | while | flops 169346176 | bytes 23139612 | solution.py:62
  71.0 6.5 %scatter_fusion = f32[29,128,128]{2,1,0:T(8,128)S(1)} fusion(f32[29,128,128]{2,1,0:T(8,128)S(1)} %broadcast.127, s32[40]{0:T(128)S(1)} %dynamic_slice.62, f32[40,128,128]{2,1,0:T(8,128)} %fusion.44), kind=kCustom, calls=%fused_computation.2.clone.clone.1 | custom fusion | flops 655360 | bytes 7864480 | tf_op jit(solution)/shard_map/while/body/eval_jaxpr/scatter-add | solution.py:58
  84.7 6.5 %scatter_fusion = f32[29,128,128]{2,1,0:T(8,128)S(1)} fusion(f32[29,128,128]{2,1,0:T(8,128)S(1)} %broadcast.127, s32[40]{0:T(128)S(1)} %dynamic_slice.62, f32[40,128,128]{2,1,0:T(8,128)} %fusion.44), kind=kCustom, calls=%fused_computation.2.clone.clone.1 | custom fusion | flops 655360 | bytes 7864480 | tf_op jit(solution)/shard_map/while/body/eval_jaxpr/scatter-add | solution.py:58
  100.0 6.5 %scatter_fusion = f32[29,128,128]{2,1,0:T(8,128)S(1)} fusion(f32[29,128,128]{2,1,0:T(8,128)S(1)} %broadcast.127, s32[40]{0:T(128)S(1)} %dynamic_slice.62, f32[40,128,128]{2,1,0:T(8,128)} %fusion.44), kind=kCustom, calls=%fused_computation.2.clone.clone.1 | custom fusion | flops 655360 | bytes 7864480 | tf_op jit(solution)/shard_map/while/body/eval_jaxpr/scatter-add | solution.py:58
  115.2 6.5 %scatter_fusion = f32[29,128,128]{2,1,0:T(8,128)S(1)} fusion(f32[29,128,128]{2,1,0:T(8,128)S(1)} %broadcast.127, s32[40]{0:T(128)S(1)} %dynamic_slice.62, f32[40,128,128]{2,1,0:T(8,128)} %fusion.44), kind=kCustom, calls=%fused_computation.2.clone.clone.1 | custom fusion | flops 655360 | bytes 7864480 | tf_op jit(solution)/shard_map/while/body/eval_jaxpr/scatter-add | solution.py:58
  130.4 6.5 %scatter_fusion = f32[29,128,128]{2,1,0:T(8,128)S(1)} fusion(f32[29,128,128]{2,1,0:T(8,128)S(1)} %broadcast.127, s32[40]{0:T(128)S(1)} %dynamic_slice.62, f32[40,128,128]{2,1,0:T(8,128)} %fusion.44), kind=kCustom, calls=%fused_computation.2.clone.clone.1 | custom fusion | flops 655360 | bytes 7864480 | tf_op jit(solution)/shard_map/while/body/eval_jaxpr/scatter-add | solution.py:58
  145.7 6.5 %scatter_fusion = f32[29,128,128]{2,1,0:T(8,128)S(1)} fusion(f32[29,128,128]{2,1,0:T(8,128)S(1)} %broadcast.127, s32[40]{0:T(128)S(1)} %dynamic_slice.62, f32[40,128,128]{2,1,0:T(8,128)} %fusion.44), kind=kCustom, calls=%fused_computation.2.clone.clone.1 | custom fusion | flops 655360 | bytes 7864480 | tf_op jit(solution)/shard_map/while/body/eval_jaxpr/scatter-add | solution.py:58
  160.9 6.5 %scatter_fusion = f32[29,128,128]{2,1,0:T(8,128)S(1)} fusion(f32[29,128,128]{2,1,0:T(8,128)S(1)} %broadcast.127, s32[40]{0:T(128)S(1)} %dynamic_slice.62, f32[40,128,128]{2,1,0:T(8,128)} %fusion.44), kind=kCustom, calls=%fused_computation.2.clone.clone.1 | custom fusion | flops 655360 | bytes 7864480 | tf_op jit(solution)/shard_map/while/body/eval_jaxpr/scatter-add | solution.py:58
  176.2 6.5 %scatter_fusion = f32[29,128,128]{2,1,0:T(8,128)S(1)} fusion(f32[29,128,128]{2,1,0:T(8,128)S(1)} %broadcast.127, s32[40]{0:T(128)S(1)} %dynamic_slice.62, f32[40,128,128]{2,1,0:T(8,128)} %fusion.44), kind=kCustom, calls=%fused_computation.2.clone.clone.1 | custom fusion | flops 655360 | bytes 7864480 | tf_op jit(solution)/shard_map/while/body/eval_jaxpr/scatter-add | solution.py:58
  187.5 14.4 %copy.13 = bf16[1,1,320,128,128]{3,4,2,1,0:T(8,128)(2,1)} copy(bf16[1,1,320,128,128]{4,3,2,1,0:T(8,128)(2,1)} %bitcast.61) | data formatting | bytes 20971520 | tf_op args[2]
  223.9 5.1 collective-permute-done.6
  236.2 113.0 %while.29 = (s32[]{:T(128)}, f32[32,128,128]{2,1,0:T(8,128)}, s32[320]{0:T(512)S(1)}, bf16[320,128,128]{1,2,0:T(8,128)(2,1)}, s32[320]{0:T(512)S(1)}, /*index=5*...) while((s32[]{:T(128)}, f32[32,128,128]{2,1,0:T(8,128)}, ...), condition=%wide.region_5.6_spmd.clone, body=%wide.region_3.5_spmd.clone.sunk | while | flops 169477248 | bytes 24188188 | solution.py:62
  240.7 6.6 %scatter_fusion.1 = f32[33,128,128]{2,1,0:T(8,128)S(1)} fusion(f32[33,128,128]{2,1,0:T(8,128)S(1)} %broadcast.134, s32[40]{0:T(128)S(1)} %dynamic_slice.65, f32[40,128,128]{2,1,0:T(8,128)} %fusion.47), kind=kCustom, calls=%fused_computation.3.clone.clone.1 | custom fusion | flops 655360 | bytes 7864480 | tf_op jit(solution)/shard_map/while/body/eval_jaxpr/scatter-add | solution.py:58
  253.5 6.6 %scatter_fusion.1 = f32[33,128,128]{2,1,0:T(8,128)S(1)} fusion(f32[33,128,128]{2,1,0:T(8,128)S(1)} %broadcast.134, s32[40]{0:T(128)S(1)} %dynamic_slice.65, f32[40,128,128]{2,1,0:T(8,128)} %fusion.47), kind=kCustom, calls=%fused_computation.3.clone.clone.1 | custom fusion | flops 655360 | bytes 7864480 | tf_op jit(solution)/shard_map/while/body/eval_jaxpr/scatter-add | solution.py:58
  267.8 6.6 %scatter_fusion.1 = f32[33,128,128]{2,1,0:T(8,128)S(1)} fusion(f32[33,128,128]{2,1,0:T(8,128)S(1)} %broadcast.134, s32[40]{0:T(128)S(1)} %dynamic_slice.65, f32[40,128,128]{2,1,0:T(8,128)} %fusion.47), kind=kCustom, calls=%fused_computation.3.clone.clone.1 | custom fusion | flops 655360 | bytes 7864480 | tf_op jit(solution)/shard_map/while/body/eval_jaxpr/scatter-add | solution.py:58
  282.2 6.6 %scatter_fusion.1 = f32[33,128,128]{2,1,0:T(8,128)S(1)} fusion(f32[33,128,128]{2,1,0:T(8,128)S(1)} %broadcast.134, s32[40]{0:T(128)S(1)} %dynamic_slice.65, f32[40,128,128]{2,1,0:T(8,128)} %fusion.47), kind=kCustom, calls=%fused_computation.3.clone.clone.1 | custom fusion | flops 655360 | bytes 7864480 | tf_op jit(solution)/shard_map/while/body/eval_jaxpr/scatter-add | solution.py:58
  296.5 6.6 %scatter_fusion.1 = f32[33,128,128]{2,1,0:T(8,128)S(1)} fusion(f32[33,128,128]{2,1,0:T(8,128)S(1)} %broadcast.134, s32[40]{0:T(128)S(1)} %dynamic_slice.65, f32[40,128,128]{2,1,0:T(8,128)} %fusion.47), kind=kCustom, calls=%fused_computation.3.clone.clone.1 | custom fusion | flops 655360 | bytes 7864480 | tf_op jit(solution)/shard_map/while/body/eval_jaxpr/scatter-add | solution.py:58
  310.8 6.6 %scatter_fusion.1 = f32[33,128,128]{2,1,0:T(8,128)S(1)} fusion(f32[33,128,128]{2,1,0:T(8,128)S(1)} %broadcast.134, s32[40]{0:T(128)S(1)} %dynamic_slice.65, f32[40,128,128]{2,1,0:T(8,128)} %fusion.47), kind=kCustom, calls=%fused_computation.3.clone.clone.1 | custom fusion | flops 655360 | bytes 7864480 | tf_op jit(solution)/shard_map/while/body/eval_jaxpr/scatter-add | solution.py:58
  325.1 6.5 %scatter_fusion.1 = f32[33,128,128]{2,1,0:T(8,128)S(1)} fusion(f32[33,128,128]{2,1,0:T(8,128)S(1)} %broadcast.134, s32[40]{0:T(128)S(1)} %dynamic_slice.65, f32[40,128,128]{2,1,0:T(8,128)} %fusion.47), kind=kCustom, calls=%fused_computation.3.clone.clone.1 | custom fusion | flops 655360 | bytes 7864480 | tf_op jit(solution)/shard_map/while/body/eval_jaxpr/scatter-add | solution.py:58
  339.4 6.5 %scatter_fusion.1 = f32[33,128,128]{2,1,0:T(8,128)S(1)} fusion(f32[33,128,128]{2,1,0:T(8,128)S(1)} %broadcast.134, s32[40]{0:T(128)S(1)} %dynamic_slice.65, f32[40,128,128]{2,1,0:T(8,128)} %fusion.47), kind=kCustom, calls=%fused_computation.3.clone.clone.1 | custom fusion | flops 655360 | bytes 7864480 | tf_op jit(solution)/shard_map/while/body/eval_jaxpr/scatter-add | solution.py:58
  351.9 75.9 %psum.15 = f32[256]{0:T(256)S(1)} all-reduce(f32[256]{0:T(256)S(1)} %get-tuple-element.296), channel_id=1, replica_groups=mesh['rep'=8,'blk'=32] {'rep','blk'}, use_global_device_ids=true, to_apply=%region_9.10 | all-reduce | flops 256 | bytes 2048 | tf_op jit(solution)/shard_map/psum | solution.py:88
  428.4 41.1 %all-reduce.2.cloned.1.call-done = f32[128,256]{1,0:T(8,128)} async-done(((f32[128,256]{1,0:T(8,128)}), f32[128,256]{1,0:T(8,128)}) %all-reduce.2.cloned.1.call-update) | async-done | bytes 131088 | tf_op jit(solution)/shard_map/psum | solution.py:88
  471.1 77.9 %reduce-scatter.2.cloned.1.call-done = bf16[512,128]{1,0:T(8,128)(2,1)} async-done(((bf16[4096,128]{1,0:T(8,128)(2,1)}), bf16[512,128]{1,0:T(8,128)(2,1)}) %reduce-scatter.2.cloned.1.call-update) | async-done | bytes 131088 | tf_op jit(solution)/shard_map/reduce_scatter | solution.py:99
  (175 shorter events, 169.6 us)
Async XLA Ops:
  7.2 208.5 %copy-start = (bf16[128,256]{1,0:T(8,128)(2,1)S(1)}, bf16[128,256]{1,0:T(8,128)(2,1)}, u32[]{:S(2)}) copy-start(bf16[128,256]{1,0:T(8,128)(2,1)} %param.19) | copy-start | bytes 196612
  7.2 58.0 %all-gather.2.cloned.1.call-start = ((), (), s32[]{:S(2)}) async-start(), calls=%async_computation.1 | async-start | bytes 1179648 | tf_op jit(solution)/shard_map/all_gather | solution.py:66
  9.6 459.9 %all-reduce.2.cloned.1.call-start = ((), (), s32[]{:S(2)}) async-start(), calls=%async_computation.3 | async-start | bytes 262144 | tf_op jit(solution)/shard_map/psum | solution.py:88
  187.4 19.5 %collective-permute-start.5 = (bf16[512,128]{1,0:T(8,128)(2,1)S(1)}, bf16[512,128]{1,0:T(8,128)(2,1)S(1)}, u32[]{:S(2)}, u32[]{:S(2)}) collective-permute-start(bf16[512,128]{1,0:T(8,128)(2,1)S(1)} %bitcast.69), channel_id=1, source_target_pairs={{0,3},{1,4},{2,5},{3,6},{4,7},{5,8},{6,9},{7,10},{8,11},{9,12},{10... | collective-permute-start | bytes 393224 | tf_op jit(solution)/shard_map/ppermute | solution.py:11
  187.5 28.0 %copy-start.1 = (bf16[512,128]{1,0:T(8,128)(2,1)S(1)}, bf16[512,128]{1,0:T(8,128)(2,1)}, u32[]{:S(2)}) copy-start(bf16[512,128]{1,0:T(8,128)(2,1)} %param.13) | copy-start | bytes 393220
  187.5 28.2 %copy-start.2 = (bf16[512,256]{1,0:T(8,128)(2,1)S(1)}, bf16[512,256]{1,0:T(8,128)(2,1)}, u32[]{:S(2)}) copy-start(bf16[512,256]{1,0:T(8,128)(2,1)} %param.21) | copy-start | bytes 786436
  187.5 28.2 %copy-start.3 = (f32[256]{0:T(256)S(1)}, f32[256]{0:T(256)}, u32[]{:S(2)}) copy-start(f32[256]{0:T(256)} %param.20) | copy-start | bytes 3076
  201.9 7.3 %collective-permute-start = (bf16[512,128]{1,0:T(8,128)(2,1)S(1)}, bf16[512,128]{1,0:T(8,128)(2,1)S(1)}, u32[]{:S(2)}, u32[]{:S(2)}) collective-permute-start(bf16[512,128]{1,0:T(8,128)(2,1)S(1)} %bitcast.68), channel_id=1, source_target_pairs={{0,29},{1,30},{2,31},{3,0},{4,1},{5,2},{6,3},{7,4},{8,5},{9,6},{10... | collective-permute-start | bytes 393224 | tf_op jit(solution)/shard_map/ppermute | solution.py:11
  203.6 9.7 %collective-permute-start.4 = (bf16[512,128]{1,0:T(8,128)(2,1)S(1)}, bf16[512,128]{1,0:T(8,128)(2,1)S(1)}, u32[]{:S(2)}, u32[]{:S(2)}) collective-permute-start(bf16[512,128]{1,0:T(8,128)(2,1)S(1)} %bitcast.67), channel_id=1, source_target_pairs={{0,2},{1,3},{2,4},{3,5},{4,6},{5,7},{6,8},{7,9},{8,10},{9,11},{10,... | collective-permute-start | bytes 393224 | tf_op jit(solution)/shard_map/ppermute | solution.py:11
  204.2 9.1 %collective-permute-start.3 = (bf16[512,128]{1,0:T(8,128)(2,1)S(1)}, bf16[512,128]{1,0:T(8,128)(2,1)S(1)}, u32[]{:S(2)}, u32[]{:S(2)}) collective-permute-start(bf16[512,128]{1,0:T(8,128)(2,1)S(1)} %bitcast.66), channel_id=1, source_target_pairs={{0,1},{1,2},{2,3},{3,4},{4,5},{5,6},{6,7},{7,8},{8,9},{9,10},{10,1... | collective-permute-start | bytes 393224 | tf_op jit(solution)/shard_map/ppermute | solution.py:11
  204.2 9.1 %collective-permute-start.2 = (bf16[512,128]{1,0:T(8,128)(2,1)S(1)}, bf16[512,128]{1,0:T(8,128)(2,1)S(1)}, u32[]{:S(2)}, u32[]{:S(2)}) collective-permute-start(bf16[512,128]{1,0:T(8,128)(2,1)S(1)} %bitcast.65), channel_id=1, source_target_pairs={{0,31},{1,0},{2,1},{3,2},{4,3},{5,4},{6,5},{7,6},{8,7},{9,8},{10,9... | collective-permute-start | bytes 393224 | tf_op jit(solution)/shard_map/ppermute | solution.py:11
  206.9 8.6 %collective-permute-start.1 = (bf16[512,128]{1,0:T(8,128)(2,1)S(1)}, bf16[512,128]{1,0:T(8,128)(2,1)S(1)}, u32[]{:S(2)}, u32[]{:S(2)}) collective-permute-start(bf16[512,128]{1,0:T(8,128)(2,1)S(1)} %bitcast.64), channel_id=1, source_target_pairs={{0,30},{1,31},{2,0},{3,1},{4,2},{5,3},{6,4},{7,5},{8,6},{9,7},{10,... | collective-permute-start | bytes 393224 | tf_op jit(solution)/shard_map/ppermute | solution.py:11
  217.0 19.1 %collective-permute-start.11 = (bf16[512,128]{1,0:T(8,128)(2,1)S(1)}, bf16[512,128]{1,0:T(8,128)(2,1)S(1)}, u32[]{:S(2)}, u32[]{:S(2)}) collective-permute-start(bf16[512,128]{1,0:T(8,128)(2,1)S(1)} %fusion.6), channel_id=1, source_target_pairs={{0,29},{1,30},{2,31},{3,0},{4,1},{5,2},{6,3},{7,4},{8,5},{9,6},{10... | collective-permute-start | bytes 393224 | tf_op jit(solution)/shard_map/ppermute | solution.py:11
  217.9 18.2 %collective-permute-start.10 = (bf16[512,128]{1,0:T(8,128)(2,1)S(1)}, bf16[512,128]{1,0:T(8,128)(2,1)S(1)}, u32[]{:S(2)}, u32[]{:S(2)}) collective-permute-start(bf16[512,128]{1,0:T(8,128)(2,1)S(1)} %fusion.6), channel_id=1, source_target_pairs={{0,30},{1,31},{2,0},{3,1},{4,2},{5,3},{6,4},{7,5},{8,6},{9,7},{10,... | collective-permute-start | bytes 393224 | tf_op jit(solution)/shard_map/ppermute | solution.py:11
  219.0 17.1 %collective-permute-start.9 = (bf16[512,128]{1,0:T(8,128)(2,1)S(1)}, bf16[512,128]{1,0:T(8,128)(2,1)S(1)}, u32[]{:S(2)}, u32[]{:S(2)}) collective-permute-start(bf16[512,128]{1,0:T(8,128)(2,1)S(1)} %fusion.6), channel_id=1, source_target_pairs={{0,31},{1,0},{2,1},{3,2},{4,3},{5,4},{6,5},{7,6},{8,7},{9,8},{10,9... | collective-permute-start | bytes 393224 | tf_op jit(solution)/shard_map/ppermute | solution.py:11
  222.3 13.7 %collective-permute-start.8 = (bf16[512,128]{1,0:T(8,128)(2,1)S(1)}, bf16[512,128]{1,0:T(8,128)(2,1)S(1)}, u32[]{:S(2)}, u32[]{:S(2)}) collective-permute-start(bf16[512,128]{1,0:T(8,128)(2,1)S(1)} %fusion.6), channel_id=1, source_target_pairs={{0,1},{1,2},{2,3},{3,4},{4,5},{5,6},{6,7},{7,8},{8,9},{9,10},{10,1... | collective-permute-start | bytes 393224 | tf_op jit(solution)/shard_map/ppermute | solution.py:11
  222.3 6.7 %collective-permute-start.6 = (bf16[512,128]{1,0:T(8,128)(2,1)S(1)}, bf16[512,128]{1,0:T(8,128)(2,1)S(1)}, u32[]{:S(2)}, u32[]{:S(2)}) collective-permute-start(bf16[512,128]{1,0:T(8,128)(2,1)S(1)} %fusion.6), channel_id=1, source_target_pairs={{0,3},{1,4},{2,5},{3,6},{4,7},{5,8},{6,9},{7,10},{8,11},{9,12},{10... | collective-permute-start | bytes 393224 | tf_op jit(solution)/shard_map/ppermute | solution.py:11
  223.9 325.1 %reduce-scatter.2.cloned.1.call-start = ((), (), s32[]{:S(2)}) async-start(), calls=%async_computation.2 | async-start | bytes 1179648 | tf_op jit(solution)/shard_map/reduce_scatter | solution.py:99
  229.0 7.0 %collective-permute-start.7 = (bf16[512,128]{1,0:T(8,128)(2,1)S(1)}, bf16[512,128]{1,0:T(8,128)(2,1)S(1)}, u32[]{:S(2)}, u32[]{:S(2)}) collective-permute-start(bf16[512,128]{1,0:T(8,128)(2,1)S(1)} %fusion.6), channel_id=1, source_target_pairs={{0,2},{1,3},{2,4},{3,5},{4,6},{5,7},{6,8},{7,9},{8,10},{9,11},{10,... | collective-permute-start | bytes 393224 | tf_op jit(solution)/shard_map/ppermute | solution.py:11
Sparse Core Ops, SparseCore 0:
  11.2 53.9 all-gather.1
  224.0 245.4 all-reduce.1
  473.4 75.5 reduce-scatter.1
where the time goes:
time: 561 us; the launch traced here: 557 us
  waiting for transfers between devices  189 us (34%)
  other arithmetic  164 us (29%)
  blocking collectives  75.9 us (14%)
  matrix products  55.7 us (10%)
  local copies, waits for them, and re-layouts  42.9 us (8%)
  between operations  14.6 us (3%)
  starting transfers between devices  14.4 us (3%)
    scatter-add x16, other arithmetic, add_block(): jax.ops.segment_sum(products, segment_part, segment_total + 1)  105 us
    reduce_scatter x1, waiting for transfers between devices, on_device(): lax.psum_scatter(column_part.reshape(rep_count * row_count, feat_width).a...  77.9 us
    psum x1, blocking collectives, on_device(): weight_sum, bias_sum = lax.psum((local_weight, local_bias), ('rep', 'blk'))  75.9 us
    dot_general x16, matrix products, add_block(): jnp.einsum(pattern, weights_part, source_tiles[gather_part], preferred_el...  53.5 us
    all_gather x1, waiting for transfers between devices, on_device(): source_rows = lax.all_gather(scaled, 'rep', axis=0, tiled=True)  53.4 us
    add x16, other arithmetic, add_block(): running + jax.ops.segment_sum(products, segment_part, segment_total + 1)[...  46.3 us
    psum x1, waiting for transfers between devices, on_device(): weight_sum, bias_sum = lax.psum((local_weight, local_bias), ('rep', 'blk'))  41.1 us
    gather x16, local copies, waits for them, and re-layouts, add_block(): source_tiles[gather_part]  22.5 us
  transfers between devices with their start and end apart: 15, of which 7 were waited for; matrix products, arithmetic and copies ran while one was open for 24% of the time, Pallas kernels for 0%

commit v1 on v0

--- a/solution.py
+++ b/solution.py
@@ -85,7 +85,7 @@
     ).astype(jnp.bfloat16)
     local_weight = jnp.dot(aggregated.T, pre_grad, preferred_element_type=jnp.float32)
     local_bias = jnp.sum(pre_grad.astype(jnp.float32), axis=0)
-    weight_sum, bias_sum = lax.psum((local_weight, local_bias), ("rep", "blk"))
+    weight_sum, bias_sum = lax.psum(lax.psum((local_weight, local_bias), "blk"), "rep")
     grad_scale = (row_count * rep_count * blk_count) ** (-0.5)
     scaled_grad = (
         node_norm[:, None] * jnp.dot(pre_grad, weight.T, preferred_element_type=jnp.float32)

time: 561 us -> 632 us (1.13)
  waiting for transfers between devices: 189 us -> 261 us
    psum x1 -> x2, waiting for transfers between devices: 41.1 us -> 197 us  [the longest x1 197 us: on_device(): lax.psum((local_weight, local_bias), 'blk')]
    reduce_scatter x1, waiting for transfers between devices: 77.9 us -> 4.42 us  [on_device(): lax.psum_scatter(column_part.reshape(rep_count * row_count, feat_width).a...]
    ppermute x12, waiting for transfers between devices: 16.3 us -> 5.64 us  [shifted(): lax.ppermute(value, axis, [(i, (i + by) % length) for i in range(length)])]
    psum x1 -> x2, blocking collectives: 75.9 us -> 73.9 us  [the longest x1 50 us: on_device(): lax.psum((local_weight, local_bias), 'blk')]
  transfers between devices with their start and end apart: 15 -> 16, of which waited for: 7 -> 4; matrix products, arithmetic and copies ran while one was open for 24% -> 21% of each run, Pallas kernels for 0% -> 0%
where the time goes in v1:
time: 632 us; the launch traced here: 627 us
  waiting for transfers between devices  261 us (41%)
  other arithmetic  164 us (26%)
  blocking collectives  73.9 us (12%)
  matrix products  55.6 us (9%)
  local copies, waits for them, and re-layouts  42.8 us (7%)
  between operations  14.7 us (2%)
  starting transfers between devices  14 us (2%)
    psum x1, waiting for transfers between devices, on_device(): lax.psum((local_weight, local_bias), 'blk')  197 us
    scatter-add x16, other arithmetic, add_block(): jax.ops.segment_sum(products, segment_part, segment_total + 1)  105 us
    all_gather x1, waiting for transfers between devices, on_device(): source_rows = lax.all_gather(scaled, 'rep', axis=0, tiled=True)  53.4 us
    dot_general x16, matrix products, add_block(): jnp.einsum(pattern, weights_part, source_tiles[gather_part], preferred_el...  53.4 us
    psum x1, blocking collectives, on_device(): lax.psum((local_weight, local_bias), 'blk')  50 us
    add x16, other arithmetic, add_block(): running + jax.ops.segment_sum(products, segment_part, segment_total + 1)[...  46.3 us
    psum x1, blocking collectives, on_device(): lax.psum(lax.psum((local_weight, local_bias), 'blk'), 'rep')  23.9 us
    gather x16, local copies, waits for them, and re-layouts, add_block(): source_tiles[gather_part]  22.5 us
  transfers between devices with their start and end apart: 16, of which 4 were waited for; matrix products, arithmetic and copies ran while one was open for 21% of the time, Pallas kernels for 0%

profile of v1, /device:TPU:32, one launch (start us, length us, event | category | flops | bytes accessed | tf_op | source)
XLA Modules:
  0.0 626.9 jit_solution(8808756606373173404)
XLA Ops:
  11.8 53.4 %all-gather.2.cloned.1.call-done = bf16[4096,128]{1,0:T(8,128)(2,1)} async-done(((bf16[512,128]{1,0:T(8,128)(2,1)}), bf16[4096,128]{1,0:T(8,128)(2,1)}) %all-gather.2.cloned.1.call-update) | async-done | bytes 1048592 | tf_op jit(solution)/shard_map/all_gather | solution.py:66
  65.2 120.4 %while.28 = (s32[]{:T(128)}, f32[28,128,128]{2,1,0:T(8,128)}, s32[320]{0:T(512)S(1)}, bf16[320,128,128]{2,1,0:T(8,128)(2,1)}, s32[320]{0:T(512)S(1)}, /*index=5*...) while((s32[]{:T(128)}, f32[28,128,128]{2,1,0:T(8,128)}, ...), condition=%wide.region_2.3_spmd.clone, body=%wide.region_0.2_spmd.clone.sunk | while | flops 169346176 | bytes 23139612 | solution.py:62
  70.9 6.5 %scatter_fusion = f32[29,128,128]{2,1,0:T(8,128)S(1)} fusion(f32[29,128,128]{2,1,0:T(8,128)S(1)} %broadcast.127, s32[40]{0:T(128)S(1)} %dynamic_slice.62, f32[40,128,128]{2,1,0:T(8,128)} %fusion.44), kind=kCustom, calls=%fused_computation.2.clone.clone.1 | custom fusion | flops 655360 | bytes 7864480 | tf_op jit(solution)/shard_map/while/body/eval_jaxpr/scatter-add | solution.py:58
  84.7 6.5 %scatter_fusion = f32[29,128,128]{2,1,0:T(8,128)S(1)} fusion(f32[29,128,128]{2,1,0:T(8,128)S(1)} %broadcast.127, s32[40]{0:T(128)S(1)} %dynamic_slice.62, f32[40,128,128]{2,1,0:T(8,128)} %fusion.44), kind=kCustom, calls=%fused_computation.2.clone.clone.1 | custom fusion | flops 655360 | bytes 7864480 | tf_op jit(solution)/shard_map/while/body/eval_jaxpr/scatter-add | solution.py:58
  99.9 6.5 %scatter_fusion = f32[29,128,128]{2,1,0:T(8,128)S(1)} fusion(f32[29,128,128]{2,1,0:T(8,128)S(1)} %broadcast.127, s32[40]{0:T(128)S(1)} %dynamic_slice.62, f32[40,128,128]{2,1,0:T(8,128)} %fusion.44), kind=kCustom, calls=%fused_computation.2.clone.clone.1 | custom fusion | flops 655360 | bytes 7864480 | tf_op jit(solution)/shard_map/while/body/eval_jaxpr/scatter-add | solution.py:58
  115.1 6.5 %scatter_fusion = f32[29,128,128]{2,1,0:T(8,128)S(1)} fusion(f32[29,128,128]{2,1,0:T(8,128)S(1)} %broadcast.127, s32[40]{0:T(128)S(1)} %dynamic_slice.62, f32[40,128,128]{2,1,0:T(8,128)} %fusion.44), kind=kCustom, calls=%fused_computation.2.clone.clone.1 | custom fusion | flops 655360 | bytes 7864480 | tf_op jit(solution)/shard_map/while/body/eval_jaxpr/scatter-add | solution.py:58
  130.4 6.5 %scatter_fusion = f32[29,128,128]{2,1,0:T(8,128)S(1)} fusion(f32[29,128,128]{2,1,0:T(8,128)S(1)} %broadcast.127, s32[40]{0:T(128)S(1)} %dynamic_slice.62, f32[40,128,128]{2,1,0:T(8,128)} %fusion.44), kind=kCustom, calls=%fused_computation.2.clone.clone.1 | custom fusion | flops 655360 | bytes 7864480 | tf_op jit(solution)/shard_map/while/body/eval_jaxpr/scatter-add | solution.py:58
  145.6 6.5 %scatter_fusion = f32[29,128,128]{2,1,0:T(8,128)S(1)} fusion(f32[29,128,128]{2,1,0:T(8,128)S(1)} %broadcast.127, s32[40]{0:T(128)S(1)} %dynamic_slice.62, f32[40,128,128]{2,1,0:T(8,128)} %fusion.44), kind=kCustom, calls=%fused_computation.2.clone.clone.1 | custom fusion | flops 655360 | bytes 7864480 | tf_op jit(solution)/shard_map/while/body/eval_jaxpr/scatter-add | solution.py:58
  160.8 6.5 %scatter_fusion = f32[29,128,128]{2,1,0:T(8,128)S(1)} fusion(f32[29,128,128]{2,1,0:T(8,128)S(1)} %broadcast.127, s32[40]{0:T(128)S(1)} %dynamic_slice.62, f32[40,128,128]{2,1,0:T(8,128)} %fusion.44), kind=kCustom, calls=%fused_computation.2.clone.clone.1 | custom fusion | flops 655360 | bytes 7864480 | tf_op jit(solution)/shard_map/while/body/eval_jaxpr/scatter-add | solution.py:58
  176.1 6.5 %scatter_fusion = f32[29,128,128]{2,1,0:T(8,128)S(1)} fusion(f32[29,128,128]{2,1,0:T(8,128)S(1)} %broadcast.127, s32[40]{0:T(128)S(1)} %dynamic_slice.62, f32[40,128,128]{2,1,0:T(8,128)} %fusion.44), kind=kCustom, calls=%fused_computation.2.clone.clone.1 | custom fusion | flops 655360 | bytes 7864480 | tf_op jit(solution)/shard_map/while/body/eval_jaxpr/scatter-add | solution.py:58
  194.2 14.4 %copy.13 = bf16[1,1,320,128,128]{3,4,2,1,0:T(8,128)(2,1)} copy(bf16[1,1,320,128,128]{4,3,2,1,0:T(8,128)(2,1)} %bitcast.61) | data formatting | bytes 20971520 | tf_op args[2]
  218.2 197.5 %all-reduce.3.cloned.1.call-done = f32[128,256]{1,0:T(8,128)} async-done(((f32[128,256]{1,0:T(8,128)}), f32[128,256]{1,0:T(8,128)}) %all-reduce.3.cloned.1.call-update) | async-done | bytes 131088 | tf_op jit(solution)/shard_map/psum | solution.py:88
  416.6 5.6 collective-permute-done.7
  422.4 113.0 %while.29 = (s32[]{:T(128)}, f32[32,128,128]{2,1,0:T(8,128)}, s32[320]{0:T(512)S(1)}, bf16[320,128,128]{1,2,0:T(8,128)(2,1)}, s32[320]{0:T(512)S(1)}, /*index=5*...) while((s32[]{:T(128)}, f32[32,128,128]{2,1,0:T(8,128)}, ...), condition=%wide.region_5.6_spmd.clone, body=%wide.region_3.5_spmd.clone.sunk | while | flops 169477248 | bytes 24188188 | solution.py:62
  427.0 6.6 %scatter_fusion.1 = f32[33,128,128]{2,1,0:T(8,128)S(1)} fusion(f32[33,128,128]{2,1,0:T(8,128)S(1)} %broadcast.134, s32[40]{0:T(128)S(1)} %dynamic_slice.65, f32[40,128,128]{2,1,0:T(8,128)} %fusion.47), kind=kCustom, calls=%fused_computation.3.clone.clone.1 | custom fusion | flops 655360 | bytes 7864480 | tf_op jit(solution)/shard_map/while/body/eval_jaxpr/scatter-add | solution.py:58
  439.8 6.6 %scatter_fusion.1 = f32[33,128,128]{2,1,0:T(8,128)S(1)} fusion(f32[33,128,128]{2,1,0:T(8,128)S(1)} %broadcast.134, s32[40]{0:T(128)S(1)} %dynamic_slice.65, f32[40,128,128]{2,1,0:T(8,128)} %fusion.47), kind=kCustom, calls=%fused_computation.3.clone.clone.1 | custom fusion | flops 655360 | bytes 7864480 | tf_op jit(solution)/shard_map/while/body/eval_jaxpr/scatter-add | solution.py:58
  454.1 6.6 %scatter_fusion.1 = f32[33,128,128]{2,1,0:T(8,128)S(1)} fusion(f32[33,128,128]{2,1,0:T(8,128)S(1)} %broadcast.134, s32[40]{0:T(128)S(1)} %dynamic_slice.65, f32[40,128,128]{2,1,0:T(8,128)} %fusion.47), kind=kCustom, calls=%fused_computation.3.clone.clone.1 | custom fusion | flops 655360 | bytes 7864480 | tf_op jit(solution)/shard_map/while/body/eval_jaxpr/scatter-add | solution.py:58
  468.4 6.6 %scatter_fusion.1 = f32[33,128,128]{2,1,0:T(8,128)S(1)} fusion(f32[33,128,128]{2,1,0:T(8,128)S(1)} %broadcast.134, s32[40]{0:T(128)S(1)} %dynamic_slice.65, f32[40,128,128]{2,1,0:T(8,128)} %fusion.47), kind=kCustom, calls=%fused_computation.3.clone.clone.1 | custom fusion | flops 655360 | bytes 7864480 | tf_op jit(solution)/shard_map/while/body/eval_jaxpr/scatter-add | solution.py:58
  482.8 6.6 %scatter_fusion.1 = f32[33,128,128]{2,1,0:T(8,128)S(1)} fusion(f32[33,128,128]{2,1,0:T(8,128)S(1)} %broadcast.134, s32[40]{0:T(128)S(1)} %dynamic_slice.65, f32[40,128,128]{2,1,0:T(8,128)} %fusion.47), kind=kCustom, calls=%fused_computation.3.clone.clone.1 | custom fusion | flops 655360 | bytes 7864480 | tf_op jit(solution)/shard_map/while/body/eval_jaxpr/scatter-add | solution.py:58
  497.1 6.5 %scatter_fusion.1 = f32[33,128,128]{2,1,0:T(8,128)S(1)} fusion(f32[33,128,128]{2,1,0:T(8,128)S(1)} %broadcast.134, s32[40]{0:T(128)S(1)} %dynamic_slice.65, f32[40,128,128]{2,1,0:T(8,128)} %fusion.47), kind=kCustom, calls=%fused_computation.3.clone.clone.1 | custom fusion | flops 655360 | bytes 7864480 | tf_op jit(solution)/shard_map/while/body/eval_jaxpr/scatter-add | solution.py:58
  511.4 6.5 %scatter_fusion.1 = f32[33,128,128]{2,1,0:T(8,128)S(1)} fusion(f32[33,128,128]{2,1,0:T(8,128)S(1)} %broadcast.134, s32[40]{0:T(128)S(1)} %dynamic_slice.65, f32[40,128,128]{2,1,0:T(8,128)} %fusion.47), kind=kCustom, calls=%fused_computation.3.clone.clone.1 | custom fusion | flops 655360 | bytes 7864480 | tf_op jit(solution)/shard_map/while/body/eval_jaxpr/scatter-add | solution.py:58
  525.7 6.5 %scatter_fusion.1 = f32[33,128,128]{2,1,0:T(8,128)S(1)} fusion(f32[33,128,128]{2,1,0:T(8,128)S(1)} %broadcast.134, s32[40]{0:T(128)S(1)} %dynamic_slice.65, f32[40,128,128]{2,1,0:T(8,128)} %fusion.47), kind=kCustom, calls=%fused_computation.3.clone.clone.1 | custom fusion | flops 655360 | bytes 7864480 | tf_op jit(solution)/shard_map/while/body/eval_jaxpr/scatter-add | solution.py:58
  538.2 50.0 %psum.30 = f32[256]{0:T(256)S(1)} all-reduce(f32[256]{0:T(256)S(1)} %get-tuple-element.296), channel_id=1, replica_groups=mesh['rep'=8,'blk'=32] {'blk'}, use_global_device_ids=true, to_apply=%region_10.11 | all-reduce | flops 256 | bytes 2048 | tf_op jit(solution)/shard_map/psum | solution.py:88
  588.2 23.9 %psum.31 = f32[256]{0:T(256)S(1)} all-reduce(f32[256]{0:T(256)S(1)} %psum.30), channel_id=1, replica_groups=mesh['rep'=8,'blk'=32] {'rep'}, use_global_device_ids=true, to_apply=%region_11.12 | all-reduce | flops 256 | bytes 2048 | tf_op jit(solution)/shard_map/psum | solution.py:88
  (179 shorter events, 162.3 us)
Async XLA Ops:
  7.2 202.7 %copy-start = (bf16[128,256]{1,0:T(8,128)(2,1)S(1)}, bf16[128,256]{1,0:T(8,128)(2,1)}, u32[]{:S(2)}) copy-start(bf16[128,256]{1,0:T(8,128)(2,1)} %param.19) | copy-start | bytes 196612
  7.2 58.0 %all-gather.2.cloned.1.call-start = ((), (), s32[]{:S(2)}) async-start(), calls=%async_computation.1 | async-start | bytes 1179648 | tf_op jit(solution)/shard_map/all_gather | solution.py:66
  9.6 406.0 %all-reduce.3.cloned.1.call-start = ((), (), s32[]{:S(2)}) async-start(), calls=%async_computation.3 | async-start | bytes 262144 | tf_op jit(solution)/shard_map/psum | solution.py:88
  187.3 5.0 collective-permute-start.5
  187.4 22.2 %collective-permute-start = (bf16[512,128]{1,0:T(8,128)(2,1)S(1)}, bf16[512,128]{1,0:T(8,128)(2,1)S(1)}, u32[]{:S(2)}, u32[]{:S(2)}) collective-permute-start(bf16[512,128]{1,0:T(8,128)(2,1)S(1)} %bitcast.68), channel_id=1, source_target_pairs={{0,29},{1,30},{2,31},{3,0},{4,1},{5,2},{6,3},{7,4},{8,5},{9,6},{10... | collective-permute-start | bytes 393224 | tf_op jit(solution)/shard_map/ppermute | solution.py:11
  189.1 20.5 %collective-permute-start.4 = (bf16[512,128]{1,0:T(8,128)(2,1)S(1)}, bf16[512,128]{1,0:T(8,128)(2,1)S(1)}, u32[]{:S(2)}, u32[]{:S(2)}) collective-permute-start(bf16[512,128]{1,0:T(8,128)(2,1)S(1)} %bitcast.67), channel_id=1, source_target_pairs={{0,2},{1,3},{2,4},{3,5},{4,6},{5,7},{6,8},{7,9},{8,10},{9,11},{10,... | collective-permute-start | bytes 393224 | tf_op jit(solution)/shard_map/ppermute | solution.py:11
  189.7 19.9 %collective-permute-start.3 = (bf16[512,128]{1,0:T(8,128)(2,1)S(1)}, bf16[512,128]{1,0:T(8,128)(2,1)S(1)}, u32[]{:S(2)}, u32[]{:S(2)}) collective-permute-start(bf16[512,128]{1,0:T(8,128)(2,1)S(1)} %bitcast.66), channel_id=1, source_target_pairs={{0,1},{1,2},{2,3},{3,4},{4,5},{5,6},{6,7},{7,8},{8,9},{9,10},{10,1... | collective-permute-start | bytes 393224 | tf_op jit(solution)/shard_map/ppermute | solution.py:11
  189.7 19.9 %collective-permute-start.2 = (bf16[512,128]{1,0:T(8,128)(2,1)S(1)}, bf16[512,128]{1,0:T(8,128)(2,1)S(1)}, u32[]{:S(2)}, u32[]{:S(2)}) collective-permute-start(bf16[512,128]{1,0:T(8,128)(2,1)S(1)} %bitcast.65), channel_id=1, source_target_pairs={{0,31},{1,0},{2,1},{3,2},{4,3},{5,4},{6,5},{7,6},{8,7},{9,8},{10,9... | collective-permute-start | bytes 393224 | tf_op jit(solution)/shard_map/ppermute | solution.py:11
  192.3 17.3 %collective-permute-start.1 = (bf16[512,128]{1,0:T(8,128)(2,1)S(1)}, bf16[512,128]{1,0:T(8,128)(2,1)S(1)}, u32[]{:S(2)}, u32[]{:S(2)}) collective-permute-start(bf16[512,128]{1,0:T(8,128)(2,1)S(1)} %bitcast.64), channel_id=1, source_target_pairs={{0,30},{1,31},{2,0},{3,1},{4,2},{5,3},{6,4},{7,5},{8,6},{9,7},{10,... | collective-permute-start | bytes 393224 | tf_op jit(solution)/shard_map/ppermute | solution.py:11
  194.2 15.4 %copy-start.1 = (bf16[512,128]{1,0:T(8,128)(2,1)S(1)}, bf16[512,128]{1,0:T(8,128)(2,1)}, u32[]{:S(2)}) copy-start(bf16[512,128]{1,0:T(8,128)(2,1)} %param.13) | copy-start | bytes 393220
  194.2 15.6 %copy-start.2 = (bf16[512,256]{1,0:T(8,128)(2,1)S(1)}, bf16[512,256]{1,0:T(8,128)(2,1)}, u32[]{:S(2)}) copy-start(bf16[512,256]{1,0:T(8,128)(2,1)} %param.21) | copy-start | bytes 786436
  194.2 15.6 %copy-start.3 = (f32[256]{0:T(256)S(1)}, f32[256]{0:T(256)}, u32[]{:S(2)}) copy-start(f32[256]{0:T(256)} %param.20) | copy-start | bytes 3076
  212.1 400.6 %all-reduce.5.cloned.1.call-start = ((), (), s32[]{:S(2)}) async-start(), calls=%async_computation.4 | async-start | bytes 262144 | tf_op jit(solution)/shard_map/psum | solution.py:88
  212.2 203.6 %collective-permute-start.6 = (bf16[512,128]{1,0:T(8,128)(2,1)S(1)}, bf16[512,128]{1,0:T(8,128)(2,1)S(1)}, u32[]{:S(2)}, u32[]{:S(2)}) collective-permute-start(bf16[512,128]{1,0:T(8,128)(2,1)S(1)} %fusion.6), channel_id=1, source_target_pairs={{0,3},{1,4},{2,5},{3,6},{4,7},{5,8},{6,9},{7,10},{8,11},{9,12},{10... | collective-permute-start | bytes 393224 | tf_op jit(solution)/shard_map/ppermute | solution.py:11
  212.3 210.2 %collective-permute-start.11 = (bf16[512,128]{1,0:T(8,128)(2,1)S(1)}, bf16[512,128]{1,0:T(8,128)(2,1)S(1)}, u32[]{:S(2)}, u32[]{:S(2)}) collective-permute-start(bf16[512,128]{1,0:T(8,128)(2,1)S(1)} %fusion.6), channel_id=1, source_target_pairs={{0,29},{1,30},{2,31},{3,0},{4,1},{5,2},{6,3},{7,4},{8,5},{9,6},{10... | collective-permute-start | bytes 393224 | tf_op jit(solution)/shard_map/ppermute | solution.py:11
  214.0 208.4 %collective-permute-start.10 = (bf16[512,128]{1,0:T(8,128)(2,1)S(1)}, bf16[512,128]{1,0:T(8,128)(2,1)S(1)}, u32[]{:S(2)}, u32[]{:S(2)}) collective-permute-start(bf16[512,128]{1,0:T(8,128)(2,1)S(1)} %fusion.6), channel_id=1, source_target_pairs={{0,30},{1,31},{2,0},{3,1},{4,2},{5,3},{6,4},{7,5},{8,6},{9,7},{10,... | collective-permute-start | bytes 393224 | tf_op jit(solution)/shard_map/ppermute | solution.py:11
  217.7 204.6 %collective-permute-start.9 = (bf16[512,128]{1,0:T(8,128)(2,1)S(1)}, bf16[512,128]{1,0:T(8,128)(2,1)S(1)}, u32[]{:S(2)}, u32[]{:S(2)}) collective-permute-start(bf16[512,128]{1,0:T(8,128)(2,1)S(1)} %fusion.6), channel_id=1, source_target_pairs={{0,31},{1,0},{2,1},{3,2},{4,3},{5,4},{6,5},{7,6},{8,7},{9,8},{10,9... | collective-permute-start | bytes 393224 | tf_op jit(solution)/shard_map/ppermute | solution.py:11
  218.2 204.0 %collective-permute-start.8 = (bf16[512,128]{1,0:T(8,128)(2,1)S(1)}, bf16[512,128]{1,0:T(8,128)(2,1)S(1)}, u32[]{:S(2)}, u32[]{:S(2)}) collective-permute-start(bf16[512,128]{1,0:T(8,128)(2,1)S(1)} %fusion.6), channel_id=1, source_target_pairs={{0,1},{1,2},{2,3},{3,4},{4,5},{5,6},{6,7},{7,8},{8,9},{9,10},{10,1... | collective-permute-start | bytes 393224 | tf_op jit(solution)/shard_map/ppermute | solution.py:11
  415.7 203.0 %reduce-scatter.2.cloned.1.call-start = ((), (), s32[]{:S(2)}) async-start(), calls=%async_computation.2 | async-start | bytes 1179648 | tf_op jit(solution)/shard_map/reduce_scatter | solution.py:99
  415.8 6.5 %collective-permute-start.7 = (bf16[512,128]{1,0:T(8,128)(2,1)S(1)}, bf16[512,128]{1,0:T(8,128)(2,1)S(1)}, u32[]{:S(2)}, u32[]{:S(2)}) collective-permute-start(bf16[512,128]{1,0:T(8,128)(2,1)S(1)} %fusion.6), channel_id=1, source_target_pairs={{0,2},{1,3},{2,4},{3,5},{4,6},{5,7},{6,8},{7,9},{8,10},{9,11},{10,... | collective-permute-start | bytes 393224 | tf_op jit(solution)/shard_map/ppermute | solution.py:11
Sparse Core Ops, SparseCore 0:
  11.2 53.9 all-gather.1
  212.2 203.4 all-reduce.2
  418.3 91.4 all-reduce.4
  538.3 80.3 reduce-scatter.1
